TPU v7x, 32 devices: a whole 2x2x4 slice. The times are simulated.
32 devices in a mesh: obs: 4 (over y, core), flux: 8 (over z, x).
Axes of the slice: x: 2, y: 2, z: 4, core: 2. Of those that a mesh axis runs over, the one named last changes fastest.
Arguments:
- jacobian: bfloat16 [512, 8192], P('obs', 'flux'), may hold values from -0.0625 to 0.0625
- probes: bfloat16 [2, 8192, 128], P(None, 'flux'), may hold values from -6 to 6
- prior_std: float32 [8192], P('flux'), may hold values from 0.5 to 2
- obs_weight: float32 [512], P('obs'), may hold values from 0.25 to 4
Outputs:
- sketch: float32 [8192, 256], P(('flux', 'obs'))
- basis_out: float32 [8192, 256], P(('flux', 'obs'))
All inputs are finite; a program needn't handle non-finite values.
Results may differ from a plain program's by a relative error of at most 0.005.
Values may be sent and summed in bfloat16 or wider, within the bound.
A program may use at most 64 MiB of HBM per device.

v0:
```python
import math
import jax
import jax.numpy as jnp
from jax import lax
from jax.sharding import PartitionSpec as P


def body(jacobian, probes, prior_std, obs_weight):
    block_count, flux_local, probe_count = probes.shape
    scaled = (probes.astype(jnp.float32) * prior_std[None, :, None]).astype(jnp.bfloat16)
    portion = flux_local // lax.axis_size("obs")
    offset = lax.axis_index("obs") * portion
    local_std = lax.dynamic_slice_in_dim(prior_std, offset, portion)
    stacked = jnp.transpose(scaled, (1, 0, 2)).reshape(flux_local, block_count * probe_count)
    forward = lax.psum(jnp.dot(jacobian, stacked, preferred_element_type=jnp.float32), "flux")
    weighted = (forward * obs_weight[:, None]).astype(jnp.bfloat16)
    adjoint = lax.psum_scatter(
        lax.dot_general(
            jacobian, weighted, (((0,), (0,)), ((), ())), preferred_element_type=jnp.float32
        ),
        "obs",
        scatter_dimension=0,
        tiled=True,
    )
    sketch = adjoint * local_std[:, None]
    gram_matrix = lax.psum(
        jnp.dot(
            sketch.T, sketch, precision=lax.Precision.HIGHEST, preferred_element_type=jnp.float32
        ),
        ("obs", "flux"),
    )
    factor = jnp.linalg.cholesky(gram_matrix)
    scale_root = math.sqrt(flux_local * lax.axis_size("flux"))
    basis_out = jax.scipy.linalg.solve_triangular(factor, sketch.T, lower=True).T * scale_root
    return (sketch, basis_out)


def solution(mesh):
    in_specs = (P("obs", "flux"), P(None, "flux", None), P("flux"), P("obs"))
    out_specs = (P(("flux", "obs"), None), P(("flux", "obs"), None))
    return jax.shard_map(body, mesh=mesh, in_specs=in_specs, out_specs=out_specs, check_vma=False)
```

profile of v0, /device:TPU:0, one launch (start us, length us, event | category | flops | bytes accessed | tf_op | source)
XLA Modules:
  0.0 313.9 jit_solution(5051485426730443432)
XLA Ops:
  7.2 0.0 copy-start
  7.2 0.0 copy-start.3
  7.2 0.0 all-reduce.4.cloned.1.call-start
  7.2 1.3 copy.10
  8.5 0.0 copy-done.3
  8.5 0.1 multiply_convert_fusion
  8.6 0.0 copy-done
  8.7 1.0 convolution_bitcast_fusion.1
  9.6 0.0 copy-start.4
  9.6 0.0 all-reduce.4.cloned.1.call-update
  9.6 0.0 reduce-scatter.2.cloned.1.call-start
  9.7 75.5 %all-reduce.4.cloned.1.call-done = f32[128,256]{0,1:T(8,128)} async-done(((f32[128,256]{0,1:T(8,128)}), f32[128,256]{0,1:T(8,128)}) %all-reduce.4.cloned.1.call-update) | async-done | bytes 131088 | tf_op jit(solution)/shard_map/psum | solution.py:15
  85.2 0.0 copy-done.4
  85.2 2.2 convolution_bitcast_fusion
  87.4 0.0 reduce-scatter.2.cloned.1.call-update
  87.4 0.0 all-reduce.6.cloned.1.call-start
  87.5 0.1 dynamic_slice.3
  87.5 24.1 %reduce-scatter.2.cloned.1.call-done = f32[256,256]{0,1:T(8,128)} async-done(((f32[1024,256]{0,1:T(8,128)}), f32[256,256]{0,1:T(8,128)}) %reduce-scatter.2.cloned.1.call-update) | async-done | bytes 262160 | tf_op jit(solution)/shard_map/reduce_scatter | solution.py:17
  111.6 1.0 broadcast_multiply_fusion
  112.6 0.8 copy.13
  113.4 1.1 fusion.11
  114.6 0.0 copy-start.2
  114.6 0.0 all-reduce.6.cloned.1.call-update
  114.6 0.9 copy-done.2
  115.5 128.9 %all-reduce.6.cloned.1.call-done = f32[256,256]{0,1:T(8,128)} async-done(((f32[256,256]{0,1:T(8,128)}), f32[256,256]{0,1:T(8,128)}) %all-reduce.6.cloned.1.call-update) | async-done | bytes 262160 | tf_op jit(solution)/shard_map/psum | solution.py:26
  244.4 0.0 copy-start.1
  244.4 1.1 copy.12
  245.6 0.0 copy-done.1
  245.6 11.7 %cholesky.50 = f32[128,128]{1,0:T(8,128)S(1)} custom-call(f32[128,128]{1,0:T(8,128)S(1)} %cholesky.118), custom_call_target="Cholesky" | custom-call | tf_op jit(solution)/shard_map/jit(cholesky)/cholesky | solution.py:32
  257.4 9.8 %custom-call.15 = f32[1,128,128]{1,2,0:T(8,128)S(1)} custom-call(f32[1,128,128]{2,1,0:T(8,128)S(1)} %get-tuple-element.27), custom_call_target="InvertDiagBlocksLowerTriangular" | custom-call | tf_op jit(solution)/shard_map/jit(cholesky)/cholesky | solution.py:32
  267.2 0.2 constant_dynamic-update-slice_fusion.1
  267.4 0.3 convolution_subtract_fusion.1
  267.7 11.7 %cholesky.105 = f32[128,128]{1,0:T(8,128)S(1)} custom-call(f32[128,128]{1,0:T(8,128)S(1)} %convolution_subtract_fusion.1), custom_call_target="Cholesky" | custom-call | tf_op jit(solution)/shard_map/jit(cholesky)/cholesky | solution.py:32
  279.5 0.7 compare_reduce_fusion
  281.6 0.1 triangular_solve.57
  281.6 4.2 %while.1 = (s32[]{:T(128)}, f32[256,256]{1,0:T(8,128)S(1)}, s32[2,2]{1,0:T(2,128)S(1)}, f32[2,128,128]{2,1,0:T(8,128)S(1)}, s32[]{:T(128)}) while((s32[]{:T(128)}, f32[256,256]{1,0:T(8,128)S(1)}, s32[2,2]{1,0:T(2,128)S(1)}, f32[2,128,128]{2,1,0:T(8,128)S(1)}, s32[]{:T(128)}) %tuple.29), condition=%wide.while_cond, body=%wide.while_body.sunk | while | flops 2 | bytes 131189 | solution.py:34
  281.8 0.6 fusion.23
  282.4 1.4 bitcast_dynamic-update-slice_fusion.2
  283.8 0.6 fusion.23
  284.4 1.4 bitcast_dynamic-update-slice_fusion.2
  285.9 19.7 %custom-call.16 = f32[2,128,128]{1,2,0:T(8,128)S(1)} custom-call(f32[2,128,128]{2,1,0:T(8,128)S(1)} %get-tuple-element.9), custom_call_target="InvertDiagBlocksLowerTriangular" | custom-call | tf_op jit(solution)/shard_map/jit(_solve_triangular)/triangular_solve | solution.py:34
  305.6 0.3 fusion.2
  305.9 0.3 convolution_subtract_fusion
  306.1 0.3 fusion.5
  306.5 0.8 copy.14
  (12 shorter events, 0.2 us)
Async XLA Ops:
  7.2 1.5 copy-start
  7.2 1.3 copy-start.3
  7.2 78.0 %all-reduce.4.cloned.1.call-start = ((), (), s32[]{:S(2)}) async-start(), calls=%async_computation.1 | async-start | bytes 262144 | tf_op jit(solution)/shard_map/psum | solution.py:15
  9.6 75.6 %copy-start.4 = (f32[128]{0:T(128)S(1)}, f32[128]{0:T(128)}, u32[]{:S(2)}) copy-start(f32[128]{0:T(128)} %param.7) | copy-start | bytes 1540
  9.6 102.0 %reduce-scatter.2.cloned.1.call-start = ((), (), s32[]{:S(2)}) async-start(), calls=%async_computation.2 | async-start | bytes 1310720 | tf_op jit(solution)/shard_map/reduce_scatter | solution.py:17
  87.4 157.0 %all-reduce.6.cloned.1.call-start = ((), (), s32[]{:S(2)}) async-start(), calls=%async_computation.3 | async-start | bytes 524288 | tf_op jit(solution)/shard_map/psum | solution.py:26
  114.6 0.9 copy-start.2
  244.4 1.2 copy-start.1
Sparse Core Ops, SparseCore 0:
  11.9 73.2 all-reduce.3
  87.7 23.8 reduce-scatter.1
  117.7 126.6 all-reduce.5
where the time goes:
time: 314 us
  waiting for transfers between devices  229 us (73%)
  other arithmetic  54.9 us (17%)
  between operations  15.3 us (5%)
  local copies, waits for them, and re-layouts  9.28 us (3%)
  matrix products  5.61 us (2%)
    psum x1, waiting for transfers between devices, body(): lax.psum(jnp.dot(sketch.T, sketch, precision=lax.Precision.HIGHEST, prefe...  129 us
    psum x1, waiting for transfers between devices, body(): lax.psum(jnp.dot(jacobian, stacked, preferred_element_type=jnp.float32),...  75.5 us
    another operation x6, other arithmetic, body(): factor = jnp.linalg.cholesky(gram_matrix)  34 us
    reduce_scatter x1, waiting for transfers between devices, body(): lax.psum_scatter(lax.dot_general(jacobian, weighted, (((0,), (0,)), ((),...  24.1 us
    another operation x3, other arithmetic, body(): jax.scipy.linalg.solve_triangular(factor, sketch.T, lower=True)  19.7 us
  transfers between devices with their start and end apart: 3, of which 3 were waited for; matrix products, arithmetic and copies ran while one was open for 0% of the time, Pallas kernels for 0%

commit v1 on v0

--- a/solution.py
+++ b/solution.py
@@ -3,6 +3,11 @@
 import jax.numpy as jnp
 from jax import lax
 from jax.sharding import PartitionSpec as P
+
+
+def _extend_axis_part(my_tile):
+    found_now = lax.psum(lax.psum(my_tile, "flux"), "obs")
+    return found_now
 
 
 def body(jacobian, probes, prior_std, obs_weight):
@@ -23,11 +28,10 @@
         tiled=True,
     )
     sketch = adjoint * local_std[:, None]
-    gram_matrix = lax.psum(
+    gram_matrix = _extend_axis_part(
         jnp.dot(
             sketch.T, sketch, precision=lax.Precision.HIGHEST, preferred_element_type=jnp.float32
-        ),
-        ("obs", "flux"),
+        )
     )
     factor = jnp.linalg.cholesky(gram_matrix)
     scale_root = math.sqrt(flux_local * lax.axis_size("flux"))

time: 314 us -> 290 us (0.924)
  waiting for transfers between devices: 229 us -> 205 us
    psum x1 -> x2, waiting for transfers between devices: 129 us -> 106 us  [_extend_axis_part(): found_now = lax.psum(lax.psum(my_tile, 'flux'), 'obs')]
  transfers between devices with their start and end apart: 3 -> 4, of which waited for: 3 -> 4; matrix products, arithmetic and copies ran while one was open for 0% -> 0% of each run, Pallas kernels for 0% -> 0%
where the time goes in v1:
time: 290 us
  waiting for transfers between devices  205 us (71%)
  other arithmetic  54.9 us (19%)
  between operations  15.3 us (5%)
  local copies, waits for them, and re-layouts  8.36 us (3%)
  matrix products  5.61 us (2%)
    psum x2, waiting for transfers between devices, _extend_axis_part(): found_now = lax.psum(lax.psum(my_tile, 'flux'), 'obs')  106 us
    psum x1, waiting for transfers between devices, body(): lax.psum(jnp.dot(jacobian, stacked, preferred_element_type=jnp.float32),...  75.5 us
    another operation x6, other arithmetic, body(): factor = jnp.linalg.cholesky(gram_matrix)  34 us
    reduce_scatter x1, waiting for transfers between devices, body(): lax.psum_scatter(lax.dot_general(jacobian, weighted, (((0,), (0,)), ((),...  24.1 us
    another operation x3, other arithmetic, body(): jax.scipy.linalg.solve_triangular(factor, sketch.T, lower=True)  19.7 us
  transfers between devices with their start and end apart: 4, of which 4 were waited for; matrix products, arithmetic and copies ran while one was open for 0% of the time, Pallas kernels for 0%

profile of v1, /device:TPU:0, one launch (start us, length us, event | category | flops | bytes accessed | tf_op | source)
XLA Modules:
  0.0 289.8 jit_solution(7751516162686516787)
XLA Ops:
  7.2 0.0 copy-start
  7.2 0.0 copy-start.3
  7.2 0.0 all-reduce.5.cloned.1.call-start
  7.2 1.3 copy.10
  8.5 0.0 copy-done.3
  8.5 0.1 multiply_convert_fusion
  8.6 0.0 copy-done
  8.7 1.0 convolution_bitcast_fusion.1
  9.6 0.0 copy-start.4
  9.6 0.0 all-reduce.5.cloned.1.call-update
  9.6 0.0 reduce-scatter.2.cloned.1.call-start
  9.7 75.5 %all-reduce.5.cloned.1.call-done = f32[128,256]{0,1:T(8,128)} async-done(((f32[128,256]{0,1:T(8,128)}), f32[128,256]{0,1:T(8,128)}) %all-reduce.5.cloned.1.call-update) | async-done | bytes 131088 | tf_op jit(solution)/shard_map/psum | solution.py:20
  85.2 0.0 copy-done.4
  85.2 2.2 convolution_bitcast_fusion
  87.4 0.0 reduce-scatter.2.cloned.1.call-update
  87.4 0.0 all-reduce.7.cloned.1.call-start
  87.4 0.1 dynamic_slice.3
  87.5 24.1 %reduce-scatter.2.cloned.1.call-done = f32[256,256]{0,1:T(8,128)} async-done(((f32[1024,256]{0,1:T(8,128)}), f32[256,256]{0,1:T(8,128)}) %reduce-scatter.2.cloned.1.call-update) | async-done | bytes 262160 | tf_op jit(solution)/shard_map/reduce_scatter | solution.py:22
  111.6 1.0 broadcast_multiply_fusion
  112.6 1.1 fusion.11
  113.7 0.0 all-reduce.7.cloned.1.call-update
  113.7 0.0 all-reduce.9.cloned.1.call-start
  113.8 0.8 copy.13
  114.7 0.0 copy-start.2
  114.7 72.0 %all-reduce.7.cloned.1.call-done = f32[256,256]{0,1:T(8,128)} async-done(((f32[256,256]{0,1:T(8,128)}), f32[256,256]{0,1:T(8,128)}) %all-reduce.7.cloned.1.call-update) | async-done | bytes 262160 | tf_op jit(solution)/shard_map/psum | solution.py:9
  186.6 0.0 all-reduce.9.cloned.1.call-update
  186.7 0.0 copy-done.2
  186.7 33.6 %all-reduce.9.cloned.1.call-done = f32[256,256]{0,1:T(8,128)} async-done(((f32[256,256]{0,1:T(8,128)}), f32[256,256]{0,1:T(8,128)}) %all-reduce.9.cloned.1.call-update) | async-done | bytes 262160 | tf_op jit(solution)/shard_map/psum | solution.py:9
  220.3 0.0 copy-start.1
  220.3 1.1 copy.12
  221.5 0.0 copy-done.1
  221.6 11.7 %cholesky.50 = f32[128,128]{1,0:T(8,128)S(1)} custom-call(f32[128,128]{1,0:T(8,128)S(1)} %cholesky.118), custom_call_target="Cholesky" | custom-call | tf_op jit(solution)/shard_map/jit(cholesky)/cholesky | solution.py:36
  233.3 9.8 %custom-call.15 = f32[1,128,128]{1,2,0:T(8,128)S(1)} custom-call(f32[1,128,128]{2,1,0:T(8,128)S(1)} %get-tuple-element.27), custom_call_target="InvertDiagBlocksLowerTriangular" | custom-call | tf_op jit(solution)/shard_map/jit(cholesky)/cholesky | solution.py:36
  243.1 0.2 constant_dynamic-update-slice_fusion.1
  243.4 0.3 convolution_subtract_fusion.1
  243.6 11.7 %cholesky.105 = f32[128,128]{1,0:T(8,128)S(1)} custom-call(f32[128,128]{1,0:T(8,128)S(1)} %convolution_subtract_fusion.1), custom_call_target="Cholesky" | custom-call | tf_op jit(solution)/shard_map/jit(cholesky)/cholesky | solution.py:36
  255.4 0.7 compare_reduce_fusion
  257.5 0.1 triangular_solve.57
  257.5 4.2 %while.1 = (s32[]{:T(128)}, f32[256,256]{1,0:T(8,128)S(1)}, s32[2,2]{1,0:T(2,128)S(1)}, f32[2,128,128]{2,1,0:T(8,128)S(1)}, s32[]{:T(128)}) while((s32[]{:T(128)}, f32[256,256]{1,0:T(8,128)S(1)}, s32[2,2]{1,0:T(2,128)S(1)}, f32[2,128,128]{2,1,0:T(8,128)S(1)}, s32[]{:T(128)}) %tuple.29), condition=%wide.while_cond, body=%wide.while_body.sunk | while | flops 2 | bytes 131189 | solution.py:38
  257.7 0.6 fusion.23
  258.3 1.4 bitcast_dynamic-update-slice_fusion.2
  259.8 0.6 fusion.23
  260.3 1.4 bitcast_dynamic-update-slice_fusion.2
  261.8 19.7 %custom-call.16 = f32[2,128,128]{1,2,0:T(8,128)S(1)} custom-call(f32[2,128,128]{2,1,0:T(8,128)S(1)} %get-tuple-element.9), custom_call_target="InvertDiagBlocksLowerTriangular" | custom-call | tf_op jit(solution)/shard_map/jit(_solve_triangular)/triangular_solve | solution.py:38
  281.5 0.3 fusion.2
  281.8 0.3 convolution_subtract_fusion
  282.1 0.3 fusion.5
  282.4 0.8 copy.14
  (12 shorter events, 0.2 us)
Async XLA Ops:
  7.2 1.5 copy-start
  7.2 1.3 copy-start.3
  7.2 78.0 %all-reduce.5.cloned.1.call-start = ((), (), s32[]{:S(2)}) async-start(), calls=%async_computation.1 | async-start | bytes 262144 | tf_op jit(solution)/shard_map/psum | solution.py:20
  9.6 75.6 %copy-start.4 = (f32[128]{0:T(128)S(1)}, f32[128]{0:T(128)}, u32[]{:S(2)}) copy-start(f32[128]{0:T(128)} %param.7) | copy-start | bytes 1540
  9.6 102.0 %reduce-scatter.2.cloned.1.call-start = ((), (), s32[]{:S(2)}) async-start(), calls=%async_computation.2 | async-start | bytes 1310720 | tf_op jit(solution)/shard_map/reduce_scatter | solution.py:22
  87.4 99.2 %all-reduce.7.cloned.1.call-start = ((), (), s32[]{:S(2)}) async-start(), calls=%async_computation.3 | async-start | bytes 524288 | tf_op jit(solution)/shard_map/psum | solution.py:9
  113.7 106.6 %all-reduce.9.cloned.1.call-start = ((), (), s32[]{:S(2)}) async-start(), calls=%async_computation.4 | async-start | bytes 524288 | tf_op jit(solution)/shard_map/psum | solution.py:9
  114.7 72.0 %copy-start.2 = (f32[256,256]{0,1:T(8,128)S(1)}, f32[256,256]{0,1:T(8,128)}, u32[]{:S(2)}) copy-start(f32[256,256]{0,1:T(8,128)} %reduce-scatter.2.cloned.1.call-done) | copy-start | bytes 786436
  220.3 1.2 copy-start.1
Sparse Core Ops, SparseCore 0:
  11.9 73.2 all-reduce.4
  87.7 23.8 reduce-scatter.1
  115.6 71.0 all-reduce.6
  188.8 31.4 all-reduce.8

commit v2 on v0

--- a/solution.py
+++ b/solution.py
@@ -3,6 +3,11 @@
 import jax.numpy as jnp
 from jax import lax
 from jax.sharding import PartitionSpec as P
+
+
+def add_all(shard, axis):
+    shards = lax.all_gather(shard, axis)
+    return jnp.sum(shards, axis=0)
 
 
 def body(jacobian, probes, prior_std, obs_weight):
@@ -23,7 +28,7 @@
         tiled=True,
     )
     sketch = adjoint * local_std[:, None]
-    gram_matrix = lax.psum(
+    gram_matrix = add_all(
         jnp.dot(
             sketch.T, sketch, precision=lax.Precision.HIGHEST, preferred_element_type=jnp.float32
         ),

time: 314 us -> 265 us (0.84)
  waiting for transfers between devices: 229 us -> 175 us
  other arithmetic: 54.9 us -> 60.5 us
    psum x1 -> x0, waiting for transfers between devices: 129 us -> none  [body(): lax.psum(jnp.dot(sketch.T, sketch, precision=lax.Precision.HIGHEST, prefe...]
    all_gather x0 -> x1, waiting for transfers between devices: none -> 76.8 us  [add_all(): shards = lax.all_gather(shard, axis)]
    reduce_sum x0 -> x1, other arithmetic: none -> 3.93 us  [add_all(): return jnp.sum(shards, axis=0)]
  transfers between devices with their start and end apart: 3 -> 3, of which waited for: 3 -> 3; matrix products, arithmetic and copies ran while one was open for 0% -> 1% of each run, Pallas kernels for 0% -> 0%
where the time goes in v2:
time: 265 us
  waiting for transfers between devices  175 us (66%)
  other arithmetic  60.5 us (23%)
  between operations  15.2 us (6%)
  local copies, waits for them, and re-layouts  8.01 us (3%)
  matrix products  5.62 us (2%)
    all_gather x1, waiting for transfers between devices, add_all(): shards = lax.all_gather(shard, axis)  76.8 us
    psum x1, waiting for transfers between devices, body(): lax.psum(jnp.dot(jacobian, stacked, preferred_element_type=jnp.float32),...  74.8 us
    another operation x6, other arithmetic, body(): factor = jnp.linalg.cholesky(gram_matrix)  34 us
    reduce_scatter x1, waiting for transfers between devices, body(): lax.psum_scatter(lax.dot_general(jacobian, weighted, (((0,), (0,)), ((),...  23.4 us
    another operation x3, other arithmetic, body(): jax.scipy.linalg.solve_triangular(factor, sketch.T, lower=True)  19.7 us
  transfers between devices with their start and end apart: 3, of which 3 were waited for; matrix products, arithmetic and copies ran while one was open for 1% of the time, Pallas kernels for 0%

profile of v2, /device:TPU:0, one launch (start us, length us, event | category | flops | bytes accessed | tf_op | source)
XLA Modules:
  0.0 264.7 jit_solution(13453754090607849242)
XLA Ops:
  7.2 0.0 copy-start
  7.2 0.0 all-reduce.3.cloned.1.call-start
  7.2 1.3 copy.13
  8.5 0.8 multiply_convert_fusion
  9.3 0.0 copy-done
  9.3 1.0 convolution_bitcast_fusion.1
  10.3 0.0 all-reduce.3.cloned.1.call-update
  10.3 0.0 reduce-scatter.2.cloned.1.call-start
  10.4 74.8 %all-reduce.3.cloned.1.call-done = f32[128,256]{0,1:T(8,128)} async-done(((f32[128,256]{0,1:T(8,128)}), f32[128,256]{0,1:T(8,128)}) %all-reduce.3.cloned.1.call-update) | async-done | bytes 131088 | tf_op jit(solution)/shard_map/psum | solution.py:20
  85.2 2.2 convolution_bitcast_fusion
  87.4 0.0 reduce-scatter.2.cloned.1.call-update
  87.4 0.0 all-gather.3.cloned.1.call-start
  87.4 0.8 dynamic_slice.3
  88.2 23.4 %reduce-scatter.2.cloned.1.call-done = f32[256,256]{0,1:T(8,128)} async-done(((f32[1024,256]{0,1:T(8,128)}), f32[256,256]{0,1:T(8,128)}) %reduce-scatter.2.cloned.1.call-update) | async-done | bytes 262160 | tf_op jit(solution)/shard_map/reduce_scatter | solution.py:22
  111.6 1.0 broadcast_multiply_fusion
  112.6 1.1 fusion.11
  113.7 0.0 all-gather.3.cloned.1.call-update
  113.8 0.8 copy.15
  114.6 1.0 fusion.21
  115.6 76.8 %all-gather.3.cloned.1.call-done = f32[8192,256]{1,0:T(8,128)} async-done(((f32[256,256]{1,0:T(8,128)}), f32[8192,256]{1,0:T(8,128)}) %all-gather.3.cloned.1.call-update) | async-done | bytes 8388624 | tf_op jit(solution)/shard_map/all_gather | solution.py:9
  192.3 3.9 %reduce_sum.9 = f32[256,256]{1,0:T(8,128)S(1)} reduce(f32[32,256,256]{2,1,0:T(8,128)} %bitcast.48, f32[]{:T(128)} %constant.87.clone.1), dimensions={0}, to_apply=%region_2.0 | reduce | flops 2031616 | bytes 8650756 | tf_op jit(solution)/shard_map/reduce_sum | solution.py:10
  196.3 0.1 copy.14
  196.5 11.7 %cholesky.50 = f32[128,128]{1,0:T(8,128)S(1)} custom-call(f32[128,128]{1,0:T(8,128)S(1)} %cholesky.118), custom_call_target="Cholesky" | custom-call | tf_op jit(solution)/shard_map/jit(cholesky)/cholesky | solution.py:37
  208.2 9.8 %custom-call.15 = f32[1,128,128]{1,2,0:T(8,128)S(1)} custom-call(f32[1,128,128]{2,1,0:T(8,128)S(1)} %get-tuple-element.29), custom_call_target="InvertDiagBlocksLowerTriangular" | custom-call | tf_op jit(solution)/shard_map/jit(cholesky)/cholesky | solution.py:37
  218.0 0.2 constant_dynamic-update-slice_fusion.1
  218.3 0.3 convolution_subtract_fusion.1
  218.5 11.7 %cholesky.105 = f32[128,128]{1,0:T(8,128)S(1)} custom-call(f32[128,128]{1,0:T(8,128)S(1)} %convolution_subtract_fusion.1), custom_call_target="Cholesky" | custom-call | tf_op jit(solution)/shard_map/jit(cholesky)/cholesky | solution.py:37
  230.3 0.7 compare_reduce_fusion
  232.4 0.1 triangular_solve.57
  232.4 4.2 %while.1 = (s32[]{:T(128)}, f32[256,256]{1,0:T(8,128)S(1)}, s32[2,2]{1,0:T(2,128)S(1)}, f32[2,128,128]{2,1,0:T(8,128)S(1)}, s32[]{:T(128)}) while((s32[]{:T(128)}, f32[256,256]{1,0:T(8,128)S(1)}, s32[2,2]{1,0:T(2,128)S(1)}, f32[2,128,128]{2,1,0:T(8,128)S(1)}, s32[]{:T(128)}) %tuple.30), condition=%wide.while_cond, body=%wide.while_body.sunk | while | flops 2 | bytes 131189 | solution.py:39
  232.6 0.6 fusion.23
  233.2 1.4 bitcast_dynamic-update-slice_fusion.2
  234.7 0.6 fusion.23
  235.2 1.4 bitcast_dynamic-update-slice_fusion.2
  236.7 19.7 %custom-call.16 = f32[2,128,128]{1,2,0:T(8,128)S(1)} custom-call(f32[2,128,128]{2,1,0:T(8,128)S(1)} %get-tuple-element.9), custom_call_target="InvertDiagBlocksLowerTriangular" | custom-call | tf_op jit(solution)/shard_map/jit(_solve_triangular)/triangular_solve | solution.py:39
  256.4 0.3 fusion.2
  256.7 0.3 convolution_subtract_fusion
  257.0 0.3 fusion.5
  257.3 0.8 copy.16
  (11 shorter events, 0.2 us)
Async XLA Ops:
  7.2 2.1 copy-start
  7.2 78.0 %all-reduce.3.cloned.1.call-start = ((), (), s32[]{:S(2)}) async-start(), calls=%async_computation.1 | async-start | bytes 262144 | tf_op jit(solution)/shard_map/psum | solution.py:20
  10.3 101.3 %reduce-scatter.2.cloned.1.call-start = ((), (), s32[]{:S(2)}) async-start(), calls=%async_computation.2 | async-start | bytes 1310720 | tf_op jit(solution)/shard_map/reduce_scatter | solution.py:22
  87.4 104.9 %all-gather.3.cloned.1.call-start = ((), (), s32[]{:S(2)}) async-start(), calls=%async_computation.3 | async-start | bytes 8650752 | tf_op jit(solution)/shard_map/all_gather | solution.py:9
Sparse Core Ops, SparseCore 0:
  11.9 73.2 all-reduce.2
  87.7 23.8 reduce-scatter.1
  115.2 77.0 all-gather.2
